TPU v7x, 512 devices: a whole 4x4x16 slice. The times are simulated.
512 devices in a mesh: row: 16 (over y, x), col: 16 (over z), depth: 2 (over core).
Axes of the slice: x: 4, y: 4, z: 16, core: 2. Of those that a mesh axis runs over, the one named last changes fastest.
Arguments:
- left_store: float32 [16, 2, 16, 2, 64, 1024], P('row', 'depth', 'col'), may hold values from -6 to 6
- left_home: int32 [16, 2, 16], P('row', 'depth'), may hold values from 0 to 15, each once within a row
- up_store: float32 [16, 2, 16, 2, 64, 1024], P('col', 'depth', 'row'), may hold values from -0.3125 to 0.3125
- up_home: int32 [16, 2, 16], P('col', 'depth'), may hold values from 0 to 15, each once within a row
- targets: int32 [16, 16, 2], P('row', 'col'), may hold values from 0 to 63, as said below
- sketch: float32 [16, 16, 2, 64, 1024], P('row', 'col'), may hold values from -0.1875 to 0.1875
Outputs:
- basis: float32 [16, 16, 2, 64, 1024], P('row', 'col', 'depth')
- weights: float32 [16, 16, 2, 64, 1024], P('row', 'col', 'depth')
Inputs may be any that keep to these rules, and one draw needn't show every extreme that they name: `left_home`: for each row and depth index the entries are the store positions 0 to 15, each once. `up_home`: for each col and depth index the entries are the store positions 0 to 15, each once. `targets`: the 2 entries of one row and col index are distinct.
All inputs are finite; a program needn't handle non-finite values.
Results may differ from a plain program's by a relative error of at most 0.0003.
Values sent between devices are 32-bit elements; how exact they have to be, the bound alone decides.
No kernel may reach another device: no remote copies, remote signals or barrier semaphores. Data moves between devices by JAX's collectives and lax.ppermute only.
A program may use at most 128 MiB of HBM per device.

v0:
```python
import math
import jax
import jax.numpy as jnp
from jax import lax
from jax.sharding import PartitionSpec as P

KD = 2
RB = 8
CB = 8


def split_up(shard, dim, devices):
    before, after = (shard.shape[:dim], shard.shape[dim + 1 :])
    return jnp.moveaxis(shard.reshape(*before, devices, -1, *after), dim, 0)


def sent_and_summed(shard, axis, dim):
    devices = lax.axis_size(axis)
    pieces = lax.all_to_all(split_up(shard, dim, devices), axis, 0, 0, tiled=True)
    return jnp.sum(pieces, axis=0)


def laid_out(pieces, dim):
    pieces = jnp.moveaxis(pieces, 0, dim)
    shape = pieces.shape
    return pieces.reshape(*shape[:dim], shape[dim] * shape[dim + 1], *shape[dim + 2 :])


def copy_for_each(shard, axis):
    devices = lax.axis_size(axis)
    return lax.all_to_all(
        jnp.broadcast_to(shard[None], (devices, *shard.shape)), axis, 0, 0, tiled=True
    )


def gathered_copies(shard, axis, dim):
    return laid_out(copy_for_each(shard, axis), dim)


def orthonormal(sample):
    gram_mat = jnp.einsum("pat,pbt->pab", sample, sample, precision=lax.Precision.HIGHEST)
    factor_low = jnp.linalg.cholesky(gram_mat)
    return lax.linalg.triangular_solve(factor_low, sample, left_side=True, lower=True)


def shards(left_store, left_home, up_store, up_home, targets, sketch):
    high = lax.Precision.HIGHEST
    left_local = left_store[0, 0]
    up_local = up_store[0, 0]
    left_table = left_home[0, 0]
    up_table = up_home[0, 0]
    left_all = lax.all_gather(left_local, "col", axis=0, tiled=True)
    up_all = lax.all_gather(up_local, "row", axis=0, tiled=True)
    left_pairs = jnp.take(left_all, left_table, axis=0)
    up_pairs = jnp.take(up_all, up_table, axis=0)
    chosen = targets[0, 0]
    block_row = chosen // CB
    block_col = chosen % CB
    row_pairs = jnp.take(left_pairs.reshape((RB, KD) + left_local.shape[1:]), block_row, axis=0)
    col_pairs = jnp.take(up_pairs.reshape((CB, KD) + up_local.shape[1:]), block_col, axis=0)
    row_basis = row_pairs[:, :, 0]
    row_coef = row_pairs[:, :, 1]
    col_coef = col_pairs[:, :, 0]
    col_basis = col_pairs[:, :, 1]
    test_rows = sketch[0, 0]
    middle = jnp.einsum("pkat,pkbt->pkab", row_coef, col_coef, precision=high)
    test_side = jnp.einsum("pat,pkbt->pkab", test_rows, col_basis, precision=high)
    folded = jnp.einsum("pkab,pkcb->pkac", test_side, middle, precision=high)
    sample_part = jnp.einsum("pkac,pkct->pat", folded, row_basis, precision=high)
    own_sketch = sent_and_summed(sample_part, "depth", 0)
    own_basis = orthonormal(own_sketch)
    bases = gathered_copies(own_basis, "depth", 0)
    inner_prod = jnp.einsum("pat,pkct->pkac", bases, row_basis, precision=high)
    turned = jnp.einsum("pkac,pkcb->pkab", inner_prod, middle, precision=high)
    project_part = jnp.einsum("pkab,pkbt->pat", turned, col_basis, precision=high)
    projected = sent_and_summed(project_part, "depth", 0)
    root_tile = math.sqrt(test_rows.shape[-1])
    return ((own_basis * root_tile)[None, None], (projected / root_tile)[None, None])


def solution(mesh):
    return jax.shard_map(
        shards,
        mesh=mesh,
        in_specs=(
            P("row", "depth", "col", None, None, None),
            P("row", "depth", None),
            P("col", "depth", "row", None, None, None),
            P("col", "depth", None),
            P("row", "col", None),
            P("row", "col", None, None, None),
        ),
        out_specs=(P("row", "col", "depth", None, None), P("row", "col", "depth", None, None)),
        check_vma=False,
    )
```

profile of v0, /device:TPU:1, one launch (start us, length us, event | category | flops | bytes accessed | tf_op | source)
XLA Modules:
  0.0 273.3 jit_solution(12288357249461976770)
XLA Ops:
  7.2 0.7 all-gather.7.cloned.1.call-update
  8.0 0.7 all-gather.5.cloned.1.call-update
  8.7 0.7 compare_select_fusion.1
  9.3 0.7 compare_and_fusion
  10.0 0.7 compare_select_fusion.3
  10.7 0.7 compare_and_fusion.1
  11.4 0.7 compare_and_fusion.3
  12.0 109.1 %all-gather.7.cloned.1.call-done = f32[16,1,1,2,64,1024]{5,4,3,2,1,0:T(8,128)} async-done(((f32[1,1,1,2,64,1024]{5,4,3,2,1,0:T(8,128)}), f32[16,1,1,2,64,1024]{5,4,3,2,1,0:T(8,128)}) %all-gather.7.cloned.1.call-update) | async-done | bytes 8388624 | tf_op jit(solution)/shard_map/all_gather | solution.py:52
  121.1 7.7 %gather_fusion.2 = f32[16,2,64,1024]{3,2,1,0:T(8,128)} fusion(f32[16,2,64,1024]{3,2,1,0:T(8,128)} %bitcast.97, s32[1024]{0:T(1024)S(1)} %pad_clamp_fusion.1), kind=kCustom, calls=%fused_computation.2.clone | custom fusion | bytes 16777280 | tf_op jit(solution)/shard_map/jit(_take)/gather | solution.py:54
  128.8 8.6 %broadcast_select_fusion = f32[16,2,64,1024]{3,2,1,0:T(8,128)} fusion(f32[16,2,64,1024]{3,2,1,0:T(8,128)} %gather_fusion.2, pred[16]{0:T(512)(128)(4,1)S(1)} %compare_and_fusion.1), kind=kLoop, calls=%fused_computation.4 | loop fusion | flops 2097152 | bytes 16777232 | tf_op jit(solution)/shard_map/jit(_take)/select_n | solution.py:54
  137.4 5.8 %gather_fusion.3 = f32[2,2,2,64,1024]{4,3,2,1,0:T(8,128)} fusion(f32[8,2,2,64,1024]{4,3,2,1,0:T(8,128)} %bitcast.94, s32[1024]{0:T(1024)S(1)} %pad_clamp_fusion), kind=kCustom, calls=%fused_computation.3.clone | custom fusion | bytes 4194312 | tf_op jit(solution)/shard_map/jit(_take)/gather | solution.py:59
  143.2 65.0 %all-gather.5.cloned.1.call-done = f32[16,1,1,2,64,1024]{5,4,3,2,1,0:T(8,128)} async-done(((f32[1,1,1,2,64,1024]{5,4,3,2,1,0:T(8,128)}), f32[16,1,1,2,64,1024]{5,4,3,2,1,0:T(8,128)}) %all-gather.5.cloned.1.call-update) | async-done | bytes 8388624 | tf_op jit(solution)/shard_map/all_gather | solution.py:53
  208.2 7.7 %gather_fusion = f32[16,2,64,1024]{3,2,1,0:T(8,128)} fusion(f32[16,2,64,1024]{3,2,1,0:T(8,128)} %bitcast.96, s32[1024]{0:T(1024)S(1)} %pad_clamp_fusion.3), kind=kCustom, calls=%fused_computation.clone | custom fusion | bytes 16777280 | tf_op jit(solution)/shard_map/jit(_take)/gather | solution.py:55
  215.8 8.6 %broadcast_select_fusion.1 = f32[16,2,64,1024]{3,2,1,0:T(8,128)} fusion(f32[16,2,64,1024]{3,2,1,0:T(8,128)} %gather_fusion, pred[16]{0:T(512)(128)(4,1)S(1)} %compare_and_fusion.3), kind=kLoop, calls=%fused_computation.5 | loop fusion | flops 2097152 | bytes 16777232 | tf_op jit(solution)/shard_map/jit(_take)/select_n | solution.py:55
  224.4 5.4 %gather_fusion.1 = f32[2,2,2,64,1024]{4,3,2,1,0:T(8,128)} fusion(f32[8,2,2,64,1024]{4,3,2,1,0:T(8,128)} %bitcast.95, s32[1024]{0:T(1024)S(1)} %pad_clamp_fusion.2), kind=kCustom, calls=%fused_computation.1.clone | custom fusion | bytes 4194312 | tf_op jit(solution)/shard_map/jit(_take)/gather | solution.py:60
  229.9 2.8 %copy_select_fusion = (f32[2,2,2,64,1024]{4,3,1,0,2:T(8,128)S(1)}, f32[2,2,2,64,1024]{4,3,1,0,2:T(8,128)S(1)}) fusion(f32[2,2,2,64,1024]{4,3,2,1,0:T(8,128)} %gather_fusion.3, pred[2]{0:T(512)(128)(4,1)S(1)} %get-tuple-element.4, f32[2,2,2,64,1024]{4,3,2,1,0:T(8,128)} %gather_fusion.1, pred[2]{0:T(512)(128)(4,1)S(1)} %get-tuple-element.8), kind=kLoop, calls=%fused_computation.6 | loop fusion | flops 1048576 | bytes 8388612 | tf_op jit(solution)/shard_map/jit(_take)/select_n | solution.py:59
  232.7 1.6 fusion.1
  234.3 1.1 fusion
  235.7 0.7 convolution_bitcast_fusion.1
  236.4 4.6 %all_to_all.15 = f32[2,1,64,1024]{3,2,1,0:T(8,128)S(1)} all-to-all(f32[2,1,64,1024]{3,2,1,0:T(8,128)S(1)} %convolution_bitcast_fusion.1), channel_id=1, replica_groups=mesh['row'=16,'col'=16,'depth'=2] {'depth'}, dimensions={0} | all-to-all | bytes 1048576 | tf_op jit(solution)/shard_map/all_to_all | solution.py:19
  241.1 0.4 fusion.10
  241.5 5.8 %custom-call.7 = f32[1,64,64]{2,1,0:T(8,128)S(1)} custom-call(f32[1,64,64]{2,1,0:T(8,128)S(1)} %fusion.6), custom_call_target="Cholesky" | custom-call | tf_op jit(solution)/shard_map/jit(cholesky)/cholesky | solution.py:42
  247.4 0.6 compare_reduce_fusion
  248.1 0.7 fusion.5
  248.7 4.9 %custom-call.8 = f32[1,1,64,64]{2,3,1,0:T(8,128)S(1)} custom-call(f32[1,1,64,64]{3,2,1,0:T(8,128)S(1)} %fusion.5), custom_call_target="InvertDiagBlocksLowerTriangular" | custom-call | tf_op jit(solution)/shard_map/triangular_solve | solution.py:43
  253.6 0.4 fusion.7
  254.1 0.7 multiply_bitcast_fusion.1
  254.8 4.2 %all_to_all.16 = f32[2,1,64,1024]{3,2,1,0:T(8,128)S(1)} all-to-all(f32[2,1,64,1024]{3,2,1,0:T(8,128)S(1)} %broadcast_in_dim.33), channel_id=1, replica_groups=mesh['row'=16,'col'=16,'depth'=2] {'depth'}, dimensions={0} | all-to-all | bytes 1048576 | tf_op jit(solution)/shard_map/all_to_all | solution.py:31
  259.0 1.6 fusion.2
  260.9 0.7 convolution_bitcast_fusion
  261.6 4.2 %all_to_all.17 = f32[2,1,64,1024]{3,2,1,0:T(8,128)S(1)} all-to-all(f32[2,1,64,1024]{3,2,1,0:T(8,128)S(1)} %convolution_bitcast_fusion), channel_id=1, replica_groups=mesh['row'=16,'col'=16,'depth'=2] {'depth'}, dimensions={0} | all-to-all | bytes 1048576 | tf_op jit(solution)/shard_map/all_to_all | solution.py:19
  265.8 0.7 multiply_bitcast_fusion
  (20 shorter events, 0.9 us)
Async XLA Ops:
  7.2 225.5 %copy-start = (f32[1,1,2,64,1024]{4,3,2,1,0:T(8,128)S(1)}, f32[1,1,2,64,1024]{4,3,2,1,0:T(8,128)}, u32[]{:S(2)}) copy-start(f32[1,1,2,64,1024]{4,3,2,1,0:T(8,128)} %param.15) | copy-start | bytes 1572868
  7.2 113.9 %all-gather.7.cloned.1.call-start = ((), (), s32[]{:S(2)}) async-start(), calls=%async_computation.4 | async-start | bytes 8912896 | tf_op jit(solution)/shard_map/all_gather | solution.py:52
  7.9 200.3 %all-gather.5.cloned.1.call-start = ((), (), s32[]{:S(2)}) async-start(), calls=%async_computation.3 | async-start | bytes 8912896 | tf_op jit(solution)/shard_map/all_gather | solution.py:53
  232.6 3.1 %copy-start.1 = (f32[2,2,2,64,1024]{4,3,1,0,2:T(8,128)}, f32[2,2,2,64,1024]{4,3,1,0,2:T(8,128)S(1)}, u32[]{:S(2)}) copy-start(f32[2,2,2,64,1024]{4,3,1,0,2:T(8,128)S(1)} %get-tuple-element.10) | copy-start | bytes 6291460
  253.6 5.4 %copy-start.2 = (f32[2,2,2,64,1024]{4,3,1,0,2:T(8,128)S(1)}, f32[2,2,2,64,1024]{4,3,1,0,2:T(8,128)}, u32[]{:S(2)}) copy-start(f32[2,2,2,64,1024]{4,3,1,0,2:T(8,128)} %copy-done.1) | copy-start | bytes 6291460
Sparse Core Ops, SparseCore 0:
  10.1 110.9 all-gather.6
  124.1 84.0 all-gather.4
where the time goes:
time: 274 us; the launch traced here: 273 us
  waiting for transfers between devices  175 us (64%)
  other arithmetic  36.9 us (13%)
  local copies, waits for them, and re-layouts  26.7 us (10%)
  between operations  14.2 us (5%)
  blocking collectives  12.9 us (5%)
  matrix products  7.07 us (3%)
    all_gather x1, waiting for transfers between devices, shards(): left_all = lax.all_gather(left_local, 'col', axis=0, tiled=True)  109 us
    all_gather x1, waiting for transfers between devices, shards(): up_all = lax.all_gather(up_local, 'row', axis=0, tiled=True)  65 us
    select_n x2, other arithmetic, shards(): left_pairs = jnp.take(left_all, left_table, axis=0)  9.27 us
    select_n x2, other arithmetic, shards(): up_pairs = jnp.take(up_all, up_table, axis=0)  9.26 us
    all_to_all x2, blocking collectives, sent_and_summed(): lax.all_to_all(split_up(shard, dim, devices), axis, 0, 0, tiled=True)  8.78 us
    gather x1, local copies, waits for them, and re-layouts, shards(): left_pairs = jnp.take(left_all, left_table, axis=0)  7.68 us
    gather x1, local copies, waits for them, and re-layouts, shards(): up_pairs = jnp.take(up_all, up_table, axis=0)  7.67 us
    another operation x3, other arithmetic, orthonormal(): factor_low = jnp.linalg.cholesky(gram_mat)  6.52 us
  transfers between devices with their start and end apart: 2, of which 2 were waited for; matrix products, arithmetic and copies ran while one was open for 9% of the time, Pallas kernels for 0%

commit v1 on v0

--- a/solution.py
+++ b/solution.py
@@ -50,7 +50,23 @@
     left_table = left_home[0, 0]
     up_table = up_home[0, 0]
     left_all = lax.all_gather(left_local, "col", axis=0, tiled=True)
-    up_all = lax.all_gather(up_local, "row", axis=0, tiled=True)
+
+    def direct_yards_all(shard_in, mesh_ax, axis_no):
+        n_parts = lax.axis_size(mesh_ax)
+        nodes = [(num, (num + 1) % n_parts) for num in range(n_parts)]
+        arrivals = [(num, (num - 1) % n_parts) for num in range(n_parts)]
+        later, inter = ([shard_in], [shard_in])
+        for _ in range(n_parts // 2):
+            later.append(lax.ppermute(later[-1], axis_name=mesh_ax, perm=nodes))
+        for _ in [*range((n_parts - 1) // 2)]:
+            inter.append(lax.ppermute(inter[-1], axis_name=mesh_ax, perm=arrivals))
+        return jnp.roll(
+            jnp.concatenate([*later[::-1], *inter[1:]], axis_no),
+            shift=(lax.axis_index(mesh_ax) - n_parts // 2) * shard_in.shape[axis_no],
+            axis=axis_no,
+        )
+
+    up_all = direct_yards_all(up_local, "row", 0)
     left_pairs = jnp.take(left_all, left_table, axis=0)
     up_pairs = jnp.take(up_all, up_table, axis=0)
     chosen = targets[0, 0]

time: 274 us -> 246 us (0.90); the launches traced: 273 us -> 242 us
  waiting for transfers between devices: 175 us -> 47.1 us
  starting transfers between devices: 0.08 us -> 66.1 us
  local copies, waits for them, and re-layouts: 26.7 us -> 43.1 us
  blocking collectives: 12.9 us -> 25 us
    all_gather x1, waiting for transfers between devices: 109 us -> 0.02 us  [shards(): left_all = lax.all_gather(left_local, 'col', axis=0, tiled=True)]
    ppermute x0 -> x15, starting transfers between devices: none -> 66.1 us  [the longest x7 46.5 us: direct_yards_all(): inter.append(lax.ppermute(inter[-1], axis_name=mesh_ax, perm=arrivals))]
    all_gather x1 -> x0, waiting for transfers between devices: 65 us -> none  [shards(): up_all = lax.all_gather(up_local, 'row', axis=0, tiled=True)]
    ppermute x0 -> x15, waiting for transfers between devices: none -> 46.4 us  [the longest x8 46.1 us: direct_yards_all(): later.append(lax.ppermute(later[-1], axis_name=mesh_ax, perm=nodes))]
    unnamed x6 -> x45, local copies, waits for them, and re-layouts: 0.03 us -> 12.7 us
    all_to_all x2, blocking collectives: 8.78 us -> 20.9 us  [sent_and_summed(): lax.all_to_all(split_up(shard, dim, devices), axis, 0, 0, tiled=True)]
    dynamic_slice x0 -> x1, local copies, waits for them, and re-layouts: none -> 4.09 us  [direct_yards_all(): jnp.roll(jnp.concatenate([*later[::-1], *inter[1:]], axis_no), shift=(lax...]
  transfers between devices with their start and end apart: 2 -> 16, of which waited for: 2 -> 9; matrix products, arithmetic and copies ran while one was open for 9% -> 19% of each run, Pallas kernels for 0% -> 0%
where the time goes in v1:
time: 246 us; the launch traced here: 242 us
  starting transfers between devices  66.1 us (27%)
  waiting for transfers between devices  47.1 us (19%)
  local copies, waits for them, and re-layouts  43.1 us (18%)
  other arithmetic  38 us (15%)
  blocking collectives  25 us (10%)
  between operations  14.6 us (6%)
  matrix products  8.32 us (3%)
    ppermute x7, starting transfers between devices, direct_yards_all(): inter.append(lax.ppermute(inter[-1], axis_name=mesh_ax, perm=arrivals))  46.5 us
    ppermute x8, waiting for transfers between devices, direct_yards_all(): later.append(lax.ppermute(later[-1], axis_name=mesh_ax, perm=nodes))  46.1 us
    all_to_all x2, blocking collectives, sent_and_summed(): lax.all_to_all(split_up(shard, dim, devices), axis, 0, 0, tiled=True)  20.9 us
    ppermute x8, starting transfers between devices, direct_yards_all(): later.append(lax.ppermute(later[-1], axis_name=mesh_ax, perm=nodes))  19.6 us
    unnamed x45, local copies, waits for them, and re-layouts  12.7 us
    select_n x2, other arithmetic, shards(): up_pairs = jnp.take(up_all, up_table, axis=0)  9.36 us
    select_n x2, other arithmetic, shards(): left_pairs = jnp.take(left_all, left_table, axis=0)  9.29 us
    gather x1, local copies, waits for them, and re-layouts, shards(): left_pairs = jnp.take(left_all, left_table, axis=0)  7.7 us
  transfers between devices with their start and end apart: 16, of which 9 were waited for; matrix products, arithmetic and copies ran while one was open for 19% of the time, Pallas kernels for 0%

profile of v1, /device:TPU:1, one launch (start us, length us, event | category | flops | bytes accessed | tf_op | source)
XLA Modules:
  0.0 242.2 jit_solution(12375369298792287076)
XLA Ops:
  7.9 3.9 %collective-permute-start = (f32[1,2,64,1024]{3,2,1,0:T(8,128)}, f32[1,2,64,1024]{3,2,1,0:T(8,128)S(1)}, u32[]{:S(2)}, u32[]{:S(2)}) collective-permute-start(f32[1,2,64,1024]{3,2,1,0:T(8,128)} %bitcast.99), channel_id=1, source_target_pairs={{0,32},{32,64},{64,96},{96,128},{128,160},{160,192},{192,224},{224... | collective-permute-start | bytes 1572872 | tf_op jit(solution)/shard_map/ppermute | solution.py:60
  11.9 10.5 %collective-permute-done = f32[1,2,64,1024]{3,2,1,0:T(8,128)S(1)} collective-permute-done((f32[1,2,64,1024]{3,2,1,0:T(8,128)}, f32[1,2,64,1024]{3,2,1,0:T(8,128)S(1)}, u32[]{:S(2)}, u32[]{:S(2)}) %collective-permute-start) | collective-permute-done | bytes 524320 | tf_op jit(solution)/shard_map/ppermute | solution.py:60
  22.4 3.5 %collective-permute-start.1 = (f32[1,2,64,1024]{3,2,1,0:T(8,128)S(1)}, f32[1,2,64,1024]{3,2,1,0:T(8,128)S(1)}, u32[]{:S(2)}, u32[]{:S(2)}) collective-permute-start(f32[1,2,64,1024]{3,2,1,0:T(8,128)S(1)} %collective-permute-done), channel_id=1, source_target_pairs={{0,32},{32,64},{64,96},{96,128},{128,160},{160,192},{192,224},{224... | collective-permute-start | bytes 1572872 | tf_op jit(solution)/shard_map/ppermute | solution.py:60
  25.9 6.5 %collective-permute-start.8 = (f32[1,2,64,1024]{3,2,1,0:T(8,128)}, f32[1,2,64,1024]{3,2,1,0:T(8,128)S(1)}, u32[]{:S(2)}, u32[]{:S(2)}) collective-permute-start(f32[1,2,64,1024]{3,2,1,0:T(8,128)} %bitcast.100), channel_id=1, source_target_pairs={{0,480},{32,0},{64,32},{96,64},{128,96},{160,128},{192,160},{224,1... | collective-permute-start | bytes 1572872 | tf_op jit(solution)/shard_map/ppermute | solution.py:62
  32.4 4.6 %collective-permute-done.1 = f32[1,2,64,1024]{3,2,1,0:T(8,128)S(1)} collective-permute-done((f32[1,2,64,1024]{3,2,1,0:T(8,128)S(1)}, f32[1,2,64,1024]{3,2,1,0:T(8,128)S(1)}, u32[]{:S(2)}, u32[]{:S(2)}) %collective-permute-start.1) | collective-permute-done | bytes 524320 | tf_op jit(solution)/shard_map/ppermute | solution.py:60
  37.0 2.6 %collective-permute-start.2 = (f32[1,2,64,1024]{3,2,1,0:T(8,128)S(1)}, f32[1,2,64,1024]{3,2,1,0:T(8,128)S(1)}, u32[]{:S(2)}, u32[]{:S(2)}) collective-permute-start(f32[1,2,64,1024]{3,2,1,0:T(8,128)S(1)} %collective-permute-done.1), channel_id=1, source_target_pairs={{0,32},{32,64},{64,96},{96,128},{128,160},{160,192},{192,224},{224... | collective-permute-start | bytes 1572872 | tf_op jit(solution)/shard_map/ppermute | solution.py:60
  39.6 6.7 %collective-permute-start.9 = (f32[1,2,64,1024]{3,2,1,0:T(8,128)S(1)}, f32[1,2,64,1024]{3,2,1,0:T(8,128)S(1)}, u32[]{:S(2)}, u32[]{:S(2)}) collective-permute-start(f32[1,2,64,1024]{3,2,1,0:T(8,128)S(1)} %collective-permute-done.8), channel_id=1, source_target_pairs={{0,480},{32,0},{64,32},{96,64},{128,96},{160,128},{192,160},{224,1... | collective-permute-start | bytes 1572872 | tf_op jit(solution)/shard_map/ppermute | solution.py:62
  46.4 4.6 %collective-permute-done.2 = f32[1,2,64,1024]{3,2,1,0:T(8,128)S(1)} collective-permute-done((f32[1,2,64,1024]{3,2,1,0:T(8,128)S(1)}, f32[1,2,64,1024]{3,2,1,0:T(8,128)S(1)}, u32[]{:S(2)}, u32[]{:S(2)}) %collective-permute-start.2) | collective-permute-done | bytes 524320 | tf_op jit(solution)/shard_map/ppermute | solution.py:60
  52.9 6.7 %collective-permute-start.10 = (f32[1,2,64,1024]{3,2,1,0:T(8,128)S(1)}, f32[1,2,64,1024]{3,2,1,0:T(8,128)}, u32[]{:S(2)}, u32[]{:S(2)}) collective-permute-start(f32[1,2,64,1024]{3,2,1,0:T(8,128)S(1)} %collective-permute-done.9), channel_id=1, source_target_pairs={{0,480},{32,0},{64,32},{96,64},{128,96},{160,128},{192,160},{224,1... | collective-permute-start | bytes 1572872 | tf_op jit(solution)/shard_map/ppermute | solution.py:62
  59.6 4.6 %collective-permute-done.3 = f32[1,2,64,1024]{3,2,1,0:T(8,128)S(1)} collective-permute-done((f32[1,2,64,1024]{3,2,1,0:T(8,128)S(1)}, f32[1,2,64,1024]{3,2,1,0:T(8,128)S(1)}, u32[]{:S(2)}, u32[]{:S(2)}) %collective-permute-start.3) | collective-permute-done | bytes 524320 | tf_op jit(solution)/shard_map/ppermute | solution.py:60
  64.2 1.9 collective-permute-start.4
  66.4 6.6 %collective-permute-start.11 = (f32[1,2,64,1024]{3,2,1,0:T(8,128)}, f32[1,2,64,1024]{3,2,1,0:T(8,128)}, u32[]{:S(2)}, u32[]{:S(2)}) collective-permute-start(f32[1,2,64,1024]{3,2,1,0:T(8,128)} %collective-permute-done.10), channel_id=1, source_target_pairs={{0,480},{32,0},{64,32},{96,64},{128,96},{160,128},{192,160},{224,1... | collective-permute-start | bytes 1572872 | tf_op jit(solution)/shard_map/ppermute | solution.py:62
  73.0 4.6 %collective-permute-done.4 = f32[1,2,64,1024]{3,2,1,0:T(8,128)} collective-permute-done((f32[1,2,64,1024]{3,2,1,0:T(8,128)S(1)}, f32[1,2,64,1024]{3,2,1,0:T(8,128)}, u32[]{:S(2)}, u32[]{:S(2)}) %collective-permute-start.4) | collective-permute-done | bytes 524320 | tf_op jit(solution)/shard_map/ppermute | solution.py:60
  80.3 6.7 %collective-permute-start.12 = (f32[1,2,64,1024]{3,2,1,0:T(8,128)}, f32[1,2,64,1024]{3,2,1,0:T(8,128)S(1)}, u32[]{:S(2)}, u32[]{:S(2)}) collective-permute-start(f32[1,2,64,1024]{3,2,1,0:T(8,128)} %collective-permute-done.11), channel_id=1, source_target_pairs={{0,480},{32,0},{64,32},{96,64},{128,96},{160,128},{192,160},{224,1... | collective-permute-start | bytes 1572872 | tf_op jit(solution)/shard_map/ppermute | solution.py:62
  87.0 5.0 %collective-permute-done.5 = f32[1,2,64,1024]{3,2,1,0:T(8,128)} collective-permute-done((f32[1,2,64,1024]{3,2,1,0:T(8,128)}, f32[1,2,64,1024]{3,2,1,0:T(8,128)}, u32[]{:S(2)}, u32[]{:S(2)}) %collective-permute-start.5) | collective-permute-done | bytes 524320 | tf_op jit(solution)/shard_map/ppermute | solution.py:60
  95.2 6.7 %collective-permute-start.13 = (f32[1,2,64,1024]{3,2,1,0:T(8,128)S(1)}, f32[1,2,64,1024]{3,2,1,0:T(8,128)S(1)}, u32[]{:S(2)}, u32[]{:S(2)}) collective-permute-start(f32[1,2,64,1024]{3,2,1,0:T(8,128)S(1)} %collective-permute-done.12), channel_id=1, source_target_pairs={{0,480},{32,0},{64,32},{96,64},{128,96},{160,128},{192,160},{224,1... | collective-permute-start | bytes 1572872 | tf_op jit(solution)/shard_map/ppermute | solution.py:62
  101.9 5.5 %collective-permute-done.6 = f32[1,2,64,1024]{3,2,1,0:T(8,128)S(1)} collective-permute-done((f32[1,2,64,1024]{3,2,1,0:T(8,128)}, f32[1,2,64,1024]{3,2,1,0:T(8,128)S(1)}, u32[]{:S(2)}, u32[]{:S(2)}) %collective-permute-start.6) | collective-permute-done | bytes 524320 | tf_op jit(solution)/shard_map/ppermute | solution.py:60
  110.6 6.7 %collective-permute-start.14 = (f32[1,2,64,1024]{3,2,1,0:T(8,128)S(1)}, f32[1,2,64,1024]{3,2,1,0:T(8,128)S(1)}, u32[]{:S(2)}, u32[]{:S(2)}) collective-permute-start(f32[1,2,64,1024]{3,2,1,0:T(8,128)S(1)} %collective-permute-done.13), channel_id=1, source_target_pairs={{0,480},{32,0},{64,32},{96,64},{128,96},{160,128},{192,160},{224,1... | collective-permute-start | bytes 1572872 | tf_op jit(solution)/shard_map/ppermute | solution.py:62
  117.3 6.7 %collective-permute-done.7 = f32[1,2,64,1024]{3,2,1,0:T(8,128)S(1)} collective-permute-done((f32[1,2,64,1024]{3,2,1,0:T(8,128)S(1)}, f32[1,2,64,1024]{3,2,1,0:T(8,128)S(1)}, u32[]{:S(2)}, u32[]{:S(2)}) %collective-permute-start.7) | collective-permute-done | bytes 524320 | tf_op jit(solution)/shard_map/ppermute | solution.py:60
  137.0 4.1 %constant_dynamic-slice_fusion = f32[16,2,64,1024]{3,2,1,0:T(8,128)} fusion(f32[32,2,64,1024]{3,2,1,0:T(8,128)S(1)} %constant_dynamic-update-slice_fusion, s32[]{:T(128)S(6)} %select_n.42), kind=kLoop, calls=%fused_computation.81 | loop fusion | bytes 16777220 | tf_op jit(solution)/shard_map/jit(_roll_dynamic)/dynamic_slice | solution.py:63
  141.0 7.7 %gather_fusion = f32[16,2,64,1024]{3,2,1,0:T(8,128)} fusion(f32[16,2,64,1024]{3,2,1,0:T(8,128)} %constant_dynamic-slice_fusion, s32[1024]{0:T(1024)S(1)} %pad_clamp_fusion.3), kind=kCustom, calls=%fused_computation.clone | custom fusion | bytes 16777280 | tf_op jit(solution)/shard_map/jit(_take)/gather | solution.py:71
  148.7 8.6 %broadcast_select_fusion.1 = f32[16,2,64,1024]{3,2,1,0:T(8,128)} fusion(f32[16,2,64,1024]{3,2,1,0:T(8,128)} %gather_fusion, pred[16]{0:T(512)(128)(4,1)S(1)} %compare_and_fusion.3), kind=kLoop, calls=%fused_computation.5 | loop fusion | flops 2097152 | bytes 16777232 | tf_op jit(solution)/shard_map/jit(_take)/select_n | solution.py:71
  157.3 5.4 %gather_fusion.1 = f32[2,2,2,64,1024]{4,3,2,1,0:T(8,128)} fusion(f32[8,2,2,64,1024]{4,3,2,1,0:T(8,128)} %bitcast.97, s32[1024]{0:T(1024)S(1)} %get-tuple-element.11), kind=kCustom, calls=%fused_computation.1.clone | custom fusion | bytes 4194312 | tf_op jit(solution)/shard_map/jit(_take)/gather | solution.py:76
  166.3 7.7 %gather_fusion.2 = f32[16,2,64,1024]{3,2,1,0:T(8,128)} fusion(f32[16,2,64,1024]{3,2,1,0:T(8,128)} %bitcast.98, s32[1024]{0:T(1024)S(1)} %pad_clamp_fusion.1), kind=kCustom, calls=%fused_computation.2.clone | custom fusion | bytes 16777280 | tf_op jit(solution)/shard_map/jit(_take)/gather | solution.py:70
  174.0 8.6 %broadcast_select_fusion = f32[16,2,64,1024]{3,2,1,0:T(8,128)} fusion(f32[16,2,64,1024]{3,2,1,0:T(8,128)} %gather_fusion.2, pred[16]{0:T(512)(128)(4,1)S(1)} %compare_and_fusion.1), kind=kLoop, calls=%fused_computation.4 | loop fusion | flops 2097152 | bytes 16777232 | tf_op jit(solution)/shard_map/jit(_take)/select_n | solution.py:70
  182.6 5.4 %gather_fusion.3 = f32[2,2,2,64,1024]{4,3,2,1,0:T(8,128)} fusion(f32[8,2,2,64,1024]{4,3,2,1,0:T(8,128)} %bitcast.96, s32[1024]{0:T(1024)S(1)} %get-tuple-element.10), kind=kCustom, calls=%fused_computation.3.clone | custom fusion | bytes 4194312 | tf_op jit(solution)/shard_map/jit(_take)/gather | solution.py:75
  192.1 16.7 %all_to_all.15 = f32[2,1,64,1024]{3,2,1,0:T(8,128)S(1)} all-to-all(f32[2,1,64,1024]{3,2,1,0:T(8,128)S(1)} %convolution_bitcast_fusion.1), channel_id=1, replica_groups=mesh['row'=16,'col'=16,'depth'=2] {'depth'}, dimensions={0} | all-to-all | bytes 1048576 | tf_op jit(solution)/shard_map/all_to_all | solution.py:19
  209.3 5.8 %custom-call.7 = f32[1,64,64]{2,1,0:T(8,128)S(1)} custom-call(f32[1,64,64]{2,1,0:T(8,128)S(1)} %fusion.6), custom_call_target="Cholesky" | custom-call | tf_op jit(solution)/shard_map/jit(cholesky)/cholesky | solution.py:42
  216.5 4.9 %custom-call.8 = f32[1,1,64,64]{2,3,1,0:T(8,128)S(1)} custom-call(f32[1,1,64,64]{3,2,1,0:T(8,128)S(1)} %fusion.5), custom_call_target="InvertDiagBlocksLowerTriangular" | custom-call | tf_op jit(solution)/shard_map/triangular_solve | solution.py:43
  222.6 4.1 %all_to_all.16 = f32[2,1,64,1024]{3,2,1,0:T(8,128)S(1)} all-to-all(f32[2,1,64,1024]{3,2,1,0:T(8,128)S(1)} %broadcast_in_dim.33), channel_id=1, replica_groups=mesh['row'=16,'col'=16,'depth'=2] {'depth'}, dimensions={0} | all-to-all | bytes 1048576 | tf_op jit(solution)/shard_map/all_to_all | solution.py:31
  226.7 2.8 %fusion.2 = f32[2,2,64,64]{2,3,1,0:T(8,128)S(1)} fusion(f32[2,2,2,64,1024]{4,3,1,0,2:T(8,128)} %copy-done.1, f32[2,1,64,1024]{3,2,1,0:T(8,128)S(1)} %all_to_all.16), kind=kOutput, calls=%fused_computation.16 | convolution fusion | flops 201326592 | bytes 1638400 | tf_op jit(solution)/shard_map/pat,pkct->pkac/dot_general | solution.py:89
  230.5 4.2 %all_to_all.17 = f32[2,1,64,1024]{3,2,1,0:T(8,128)S(1)} all-to-all(f32[2,1,64,1024]{3,2,1,0:T(8,128)S(1)} %convolution_bitcast_fusion), channel_id=1, replica_groups=mesh['row'=16,'col'=16,'depth'=2] {'depth'}, dimensions={0} | all-to-all | bytes 1048576 | tf_op jit(solution)/shard_map/all_to_all | solution.py:19
  (88 shorter events, 36.9 us)
Async XLA Ops:
  7.2 157.5 %copy-start = (f32[1,1,2,64,1024]{4,3,2,1,0:T(8,128)S(1)}, f32[1,1,2,64,1024]{4,3,2,1,0:T(8,128)}, u32[]{:S(2)}) copy-start(f32[1,1,2,64,1024]{4,3,2,1,0:T(8,128)} %param.15) | copy-start | bytes 1572868
  7.2 127.3 %copy-start.2 = (f32[1,1,1,2,64,1024]{5,4,3,2,1,0:T(8,128)S(1)}, f32[1,1,1,2,64,1024]{5,4,3,2,1,0:T(8,128)}, u32[]{:S(2)}) copy-start(f32[1,1,1,2,64,1024]{5,4,3,2,1,0:T(8,128)} %param.12) | copy-start | bytes 1572868
  7.2 159.1 %all-gather.3.cloned.1.call-start = ((), (), s32[]{:S(2)}) async-start(), calls=%async_computation.3 | async-start | bytes 8912896 | tf_op jit(solution)/shard_map/all_gather | solution.py:52
  7.9 14.4 %collective-permute-start = (f32[1,2,64,1024]{3,2,1,0:T(8,128)}, f32[1,2,64,1024]{3,2,1,0:T(8,128)S(1)}, u32[]{:S(2)}, u32[]{:S(2)}) collective-permute-start(f32[1,2,64,1024]{3,2,1,0:T(8,128)} %bitcast.99), channel_id=1, source_target_pairs={{0,32},{32,64},{64,96},{96,128},{128,160},{160,192},{192,224},{224... | collective-permute-start | bytes 1572872 | tf_op jit(solution)/shard_map/ppermute | solution.py:60
  22.4 14.7 %collective-permute-start.1 = (f32[1,2,64,1024]{3,2,1,0:T(8,128)S(1)}, f32[1,2,64,1024]{3,2,1,0:T(8,128)S(1)}, u32[]{:S(2)}, u32[]{:S(2)}) collective-permute-start(f32[1,2,64,1024]{3,2,1,0:T(8,128)S(1)} %collective-permute-done), channel_id=1, source_target_pairs={{0,32},{32,64},{64,96},{96,128},{128,160},{160,192},{192,224},{224... | collective-permute-start | bytes 1572872 | tf_op jit(solution)/shard_map/ppermute | solution.py:60
  25.9 13.7 %collective-permute-start.8 = (f32[1,2,64,1024]{3,2,1,0:T(8,128)}, f32[1,2,64,1024]{3,2,1,0:T(8,128)S(1)}, u32[]{:S(2)}, u32[]{:S(2)}) collective-permute-start(f32[1,2,64,1024]{3,2,1,0:T(8,128)} %bitcast.100), channel_id=1, source_target_pairs={{0,480},{32,0},{64,32},{96,64},{128,96},{160,128},{192,160},{224,1... | collective-permute-start | bytes 1572872 | tf_op jit(solution)/shard_map/ppermute | solution.py:62
  37.0 13.9 %collective-permute-start.2 = (f32[1,2,64,1024]{3,2,1,0:T(8,128)S(1)}, f32[1,2,64,1024]{3,2,1,0:T(8,128)S(1)}, u32[]{:S(2)}, u32[]{:S(2)}) collective-permute-start(f32[1,2,64,1024]{3,2,1,0:T(8,128)S(1)} %collective-permute-done.1), channel_id=1, source_target_pairs={{0,32},{32,64},{64,96},{96,128},{128,160},{160,192},{192,224},{224... | collective-permute-start | bytes 1572872 | tf_op jit(solution)/shard_map/ppermute | solution.py:60
  39.6 13.3 %collective-permute-start.9 = (f32[1,2,64,1024]{3,2,1,0:T(8,128)S(1)}, f32[1,2,64,1024]{3,2,1,0:T(8,128)S(1)}, u32[]{:S(2)}, u32[]{:S(2)}) collective-permute-start(f32[1,2,64,1024]{3,2,1,0:T(8,128)S(1)} %collective-permute-done.8), channel_id=1, source_target_pairs={{0,480},{32,0},{64,32},{96,64},{128,96},{160,128},{192,160},{224,1... | collective-permute-start | bytes 1572872 | tf_op jit(solution)/shard_map/ppermute | solution.py:62
  51.0 15.4 %copy-start.3 = (f32[1,2,64,1024]{3,2,1,0:T(8,128)}, f32[1,2,64,1024]{3,2,1,0:T(8,128)S(1)}, u32[]{:S(2)}) copy-start(f32[1,2,64,1024]{3,2,1,0:T(8,128)S(1)} %collective-permute-done.2) | copy-start | bytes 1572868
  51.0 13.2 %collective-permute-start.3 = (f32[1,2,64,1024]{3,2,1,0:T(8,128)S(1)}, f32[1,2,64,1024]{3,2,1,0:T(8,128)S(1)}, u32[]{:S(2)}, u32[]{:S(2)}) collective-permute-start(f32[1,2,64,1024]{3,2,1,0:T(8,128)S(1)} %collective-permute-done.2), channel_id=1, source_target_pairs={{0,32},{32,64},{64,96},{96,128},{128,160},{160,192},{192,224},{224... | collective-permute-start | bytes 1572872 | tf_op jit(solution)/shard_map/ppermute | solution.py:60
  52.9 13.5 %collective-permute-start.10 = (f32[1,2,64,1024]{3,2,1,0:T(8,128)S(1)}, f32[1,2,64,1024]{3,2,1,0:T(8,128)}, u32[]{:S(2)}, u32[]{:S(2)}) collective-permute-start(f32[1,2,64,1024]{3,2,1,0:T(8,128)S(1)} %collective-permute-done.9), channel_id=1, source_target_pairs={{0,480},{32,0},{64,32},{96,64},{128,96},{160,128},{192,160},{224,1... | collective-permute-start | bytes 1572872 | tf_op jit(solution)/shard_map/ppermute | solution.py:62
  64.2 8.7 %copy-start.5 = (f32[1,2,64,1024]{3,2,1,0:T(8,128)}, f32[1,2,64,1024]{3,2,1,0:T(8,128)S(1)}, u32[]{:S(2)}) copy-start(f32[1,2,64,1024]{3,2,1,0:T(8,128)S(1)} %collective-permute-done.3) | copy-start | bytes 1572868
  64.2 13.3 %collective-permute-start.4 = (f32[1,2,64,1024]{3,2,1,0:T(8,128)S(1)}, f32[1,2,64,1024]{3,2,1,0:T(8,128)}, u32[]{:S(2)}, u32[]{:S(2)}) collective-permute-start(f32[1,2,64,1024]{3,2,1,0:T(8,128)S(1)} %collective-permute-done.3), channel_id=1, source_target_pairs={{0,32},{32,64},{64,96},{96,128},{128,160},{160,192},{192,224},{224... | collective-permute-start | bytes 1572872 | tf_op jit(solution)/shard_map/ppermute | solution.py:60
  66.4 13.9 %collective-permute-start.11 = (f32[1,2,64,1024]{3,2,1,0:T(8,128)}, f32[1,2,64,1024]{3,2,1,0:T(8,128)}, u32[]{:S(2)}, u32[]{:S(2)}) collective-permute-start(f32[1,2,64,1024]{3,2,1,0:T(8,128)} %collective-permute-done.10), channel_id=1, source_target_pairs={{0,480},{32,0},{64,32},{96,64},{128,96},{160,128},{192,160},{224,1... | collective-permute-start | bytes 1572872 | tf_op jit(solution)/shard_map/ppermute | solution.py:62
  77.6 14.4 %collective-permute-start.5 = (f32[1,2,64,1024]{3,2,1,0:T(8,128)}, f32[1,2,64,1024]{3,2,1,0:T(8,128)}, u32[]{:S(2)}, u32[]{:S(2)}) collective-permute-start(f32[1,2,64,1024]{3,2,1,0:T(8,128)} %collective-permute-done.4), channel_id=1, source_target_pairs={{0,32},{32,64},{64,96},{96,128},{128,160},{160,192},{192,224},{224... | collective-permute-start | bytes 1572872 | tf_op jit(solution)/shard_map/ppermute | solution.py:60
  79.5 54.8 %copy-start.6 = (f32[1,2,64,1024]{3,2,1,0:T(8,128)S(1)}, f32[1,2,64,1024]{3,2,1,0:T(8,128)}, u32[]{:S(2)}) copy-start(f32[1,2,64,1024]{3,2,1,0:T(8,128)} %copy-done.5) | copy-start | bytes 1572868
  79.5 54.8 %copy-start.4 = (f32[1,2,64,1024]{3,2,1,0:T(8,128)S(1)}, f32[1,2,64,1024]{3,2,1,0:T(8,128)}, u32[]{:S(2)}) copy-start(f32[1,2,64,1024]{3,2,1,0:T(8,128)} %copy-done.3) | copy-start | bytes 1572868
  80.3 14.9 %collective-permute-start.12 = (f32[1,2,64,1024]{3,2,1,0:T(8,128)}, f32[1,2,64,1024]{3,2,1,0:T(8,128)S(1)}, u32[]{:S(2)}, u32[]{:S(2)}) collective-permute-start(f32[1,2,64,1024]{3,2,1,0:T(8,128)} %collective-permute-done.11), channel_id=1, source_target_pairs={{0,480},{32,0},{64,32},{96,64},{128,96},{160,128},{192,160},{224,1... | collective-permute-start | bytes 1572872 | tf_op jit(solution)/shard_map/ppermute | solution.py:62
  91.9 15.4 %collective-permute-start.6 = (f32[1,2,64,1024]{3,2,1,0:T(8,128)}, f32[1,2,64,1024]{3,2,1,0:T(8,128)S(1)}, u32[]{:S(2)}, u32[]{:S(2)}) collective-permute-start(f32[1,2,64,1024]{3,2,1,0:T(8,128)} %collective-permute-done.5), channel_id=1, source_target_pairs={{0,32},{32,64},{64,96},{96,128},{128,160},{160,192},{192,224},{224... | collective-permute-start | bytes 1572872 | tf_op jit(solution)/shard_map/ppermute | solution.py:60
  95.2 15.4 %collective-permute-start.13 = (f32[1,2,64,1024]{3,2,1,0:T(8,128)S(1)}, f32[1,2,64,1024]{3,2,1,0:T(8,128)S(1)}, u32[]{:S(2)}, u32[]{:S(2)}) collective-permute-start(f32[1,2,64,1024]{3,2,1,0:T(8,128)S(1)} %collective-permute-done.12), channel_id=1, source_target_pairs={{0,480},{32,0},{64,32},{96,64},{128,96},{160,128},{192,160},{224,1... | collective-permute-start | bytes 1572872 | tf_op jit(solution)/shard_map/ppermute | solution.py:62
  107.4 16.7 %collective-permute-start.7 = (f32[1,2,64,1024]{3,2,1,0:T(8,128)S(1)}, f32[1,2,64,1024]{3,2,1,0:T(8,128)S(1)}, u32[]{:S(2)}, u32[]{:S(2)}) collective-permute-start(f32[1,2,64,1024]{3,2,1,0:T(8,128)S(1)} %collective-permute-done.6), channel_id=1, source_target_pairs={{0,32},{32,64},{64,96},{96,128},{128,160},{160,192},{192,224},{224... | collective-permute-start | bytes 1572872 | tf_op jit(solution)/shard_map/ppermute | solution.py:60
  110.6 21.4 %collective-permute-start.14 = (f32[1,2,64,1024]{3,2,1,0:T(8,128)S(1)}, f32[1,2,64,1024]{3,2,1,0:T(8,128)S(1)}, u32[]{:S(2)}, u32[]{:S(2)}) collective-permute-start(f32[1,2,64,1024]{3,2,1,0:T(8,128)S(1)} %collective-permute-done.13), channel_id=1, source_target_pairs={{0,480},{32,0},{64,32},{96,64},{128,96},{160,128},{192,160},{224,1... | collective-permute-start | bytes 1572872 | tf_op jit(solution)/shard_map/ppermute | solution.py:62
  189.9 1.5 copy-start.1
Sparse Core Ops, SparseCore 0:
  10.1 110.9 all-gather.2
